TPU v7x, 512 devices: a whole 4x8x8 slice. The times are simulated.
512 devices in a mesh: node: 32 (over z, x_lo, core), local: 16 (over x_hi, y).
Axes of the slice: x: 4 (x_hi: 2, x_lo: 2; x = x_hi * 2 + x_lo), y: 8, z: 8, core: 2. Of those that a mesh axis runs over, the one named last changes fastest.
Arguments:
- tokens: bfloat16 [2048, 4096], P('local', 'node'), may hold values from -6 to 6
- gate_up_codes: bfloat16 [2, 4096, 14336], P(None, 'local', 'node'), may hold values from -127 to 127
- gate_up_scales: bfloat16 [2, 32, 14336], P(None, 'local', 'node'), may hold values from 2.9921532e-05 to 0.00029945374
- d_hidden: bfloat16 [2048, 14336], P('local', 'node'), may hold values from -6 to 6
Outputs:
- hidden: bfloat16 [2048, 14336], P('local', 'node')
- d_tokens: bfloat16 [2048, 4096], P('local', 'node')
- grad_gate_up: float32 [2, 4096, 14336], P(None, 'local', 'node')
All inputs are finite; a program needn't handle non-finite values.
Results may differ from a plain program's by a relative error of at most 0.023.
Values may be sent and summed in bfloat16 or wider, within the bound.
A program may use at most 128 MiB of HBM per device.

v0:
```python
import math

import jax
import jax.numpy as jnp
from jax import lax
from jax.sharding import PartitionSpec as P

BLOCK = 128


def from_everyone(array, axis):
    length = lax.axis_size(axis)
    return lax.all_to_all(
        jnp.broadcast_to(array[None], (length, *array.shape)), axis, 0, 0, tiled=True
    )


def in_order(pieces, dim):
    pieces = jnp.moveaxis(pieces, 0, dim)
    lengths = pieces.shape
    return pieces.reshape(*lengths[:dim], lengths[dim] * lengths[dim + 1], *lengths[dim + 2 :])


def gather_directly(array, axis, dim):
    pieces = from_everyone(array, axis)
    return in_order(pieces, dim)


def cut_along(array, dim, length):
    before, after = (array.shape[:dim], array.shape[dim + 1 :])
    return jnp.moveaxis(array.reshape(*before, length, -1, *after), dim, 0)


def sent_and_summed(array, axis, dim):
    pieces = cut_along(array, dim, lax.axis_size(axis))
    arrived = lax.all_to_all(pieces, axis, split_axis=0, concat_axis=0, tiled=True)
    return arrived.astype(jnp.float32).sum(axis=0)


def sent_together(arrays, axis, dim, along):
    both = jnp.concatenate(arrays, axis=along)
    out, at, outs = (lax.all_gather(both, axis, axis=dim, tiled=True), 0, [])
    for a in arrays:
        outs.append(lax.slice_in_dim(out, at, at + a.shape[along], axis=along))
        at += a.shape[along]
    return tuple(outs)


def dequant(codes, scales):
    shape = codes.shape
    blocked = codes.astype(jnp.float32).reshape(shape[:-2] + (shape[-2] // BLOCK, BLOCK, shape[-1]))
    weight = blocked * scales.astype(jnp.float32)[..., :, None, :]
    return weight.reshape(shape).astype(jnp.bfloat16)


def body(tokens, gate_up_codes, gate_up_scales, d_hidden):
    rows = tokens.shape[0]
    local_count = lax.axis_size("local")
    features = gather_directly(tokens, "node", 1)
    width = features.shape[1]
    all_codes, all_scales = (
        lax.all_gather(gate_up_codes, "local", axis=1, tiled=True),
        lax.all_gather(gate_up_scales, "local", axis=1, tiled=True),
    )
    w_gu = dequant(all_codes, all_scales)
    group = w_gu.shape[2]
    gate = jnp.dot(features, w_gu[0], preferred_element_type=jnp.float32)
    up = jnp.dot(features, w_gu[1], preferred_element_type=jnp.float32)
    sigmoid_gate = jax.nn.sigmoid(gate)
    active = gate * sigmoid_gate
    hidden = (active * up).astype(jnp.bfloat16)
    grad_in = d_hidden.astype(jnp.float32)
    d_gate = (grad_in * up * sigmoid_gate * (1.0 + gate * (1.0 - sigmoid_gate))).astype(
        jnp.bfloat16
    )
    d_up = (grad_in * active).astype(jnp.bfloat16)
    term = lax.dot_general(
        d_gate, w_gu[0], (((1,), (1,)), ((), ())), preferred_element_type=jnp.float32
    )
    term = term + lax.dot_general(
        d_up, w_gu[1], (((1,), (1,)), ((), ())), preferred_element_type=jnp.float32
    )
    rounded = lax.optimization_barrier(term.astype(jnp.bfloat16)).astype(jnp.float32)
    d_tokens = sent_and_summed(rounded.astype(jnp.bfloat16), "node", 1).astype(jnp.bfloat16)
    factor = 1.0 / math.sqrt(rows * local_count)
    owned = width // local_count
    columns = lax.all_to_all(features, "local", split_axis=1, concat_axis=0, tiled=True)
    gate_all, up_all = sent_together((d_gate, d_up), "local", 0, 1)
    both_all = jnp.concatenate(
        [gate_all.reshape(local_count, rows, group), up_all.reshape(local_count, rows, group)],
        axis=2,
    )
    blocks = columns.reshape(local_count, rows, owned)
    numbers = (((1,), (1,)), ((0,), (0,)))
    partial_value = lax.dot_general(
        blocks, both_all, numbers, preferred_element_type=jnp.float32
    ).astype(jnp.bfloat16)
    summed = jnp.sum(partial_value.astype(jnp.float32), axis=0) * factor
    grads = summed.reshape(owned, 2, group).transpose(1, 0, 2)
    return (hidden, d_tokens, grads)


def solution(mesh):
    placed = (
        P("local", "node"),
        P(None, "local", "node"),
        P(None, "local", "node"),
        P("local", "node"),
    )
    return jax.shard_map(
        body,
        mesh=mesh,
        in_specs=placed,
        out_specs=(P("local", "node"), P("local", "node"), P(None, "local", "node")),
        check_vma=False,
    )
```

profile of v0, /device:TPU:1, one launch (start us, length us, event | category | flops | bytes accessed | tf_op | source)
XLA Modules:
  0.0 307.7 jit_solution(12713937167241401182)
XLA Ops:
  7.9 0.9 copy.25
  8.8 1.3 broadcast_in_dim.2
  10.1 12.9 %all-to-all-start = ((bf16[32,128,128]{1,2,0:T(8,128)(2,1)}), bf16[32,128,128]{1,2,0:T(8,128)(2,1)S(1)}, u32[]{:S(2)}, u32[]{:S(2)}) async-start(bf16[32,128,128]{1,2,0:T(8,128)(2,1)} %broadcast_in_dim.2), calls=%async_computation | async-start | bytes 2097152 | tf_op jit(solution)/shard_map/all_to_all | solution.py:13
  23.0 35.1 %all_gather.10 = bf16[2,32,448]{2,0,1:T(2,128)(2,1)S(1)} all-gather(bf16[2,2,448]{2,0,1:T(2,128)(2,1)S(1)} %copy.22), channel_id=1, replica_groups=mesh['node'=32,'local'=16] {'local'}, dimensions={1}, use_global_device_ids=true | all-gather | bytes 60928 | tf_op jit(solution)/shard_map/all_gather | solution.py:63
  58.4 7.9 %mul.45 = f32[2,32,128,448]{2,1,3,0:T(8,128)} broadcast(f32[2,32,448]{1,2,0:T(8,128)S(1)} %copy.24), dimensions={0,1,3} | broadcast | bytes 14794752 | tf_op jit(solution)/shard_map/mul | solution.py:52
  66.2 16.0 %mul.46 = f32[2,4096,448]{1,2,0:T(8,128)} reshape(f32[2,32,128,448]{2,1,3,0:T(8,128)} %mul.45) | data formatting | bytes 29360128 | tf_op jit(solution)/shard_map/mul | solution.py:52
  82.3 75.9 %all-gather.3.cloned.1.call-done = bf16[2,4096,448]{1,2,0:T(8,128)(2,1)} async-done(((bf16[2,256,448]{1,2,0:T(8,128)(2,1)}), bf16[2,4096,448]{1,2,0:T(8,128)(2,1)}) %all-gather.3.cloned.1.call-update) | async-done | bytes 7340048 | tf_op jit(solution)/shard_map/all_gather | solution.py:62
  158.2 10.6 %multiply_convert_fusion = bf16[2,4096,448]{1,2,0:T(8,128)(2,1)} fusion(f32[2,4096,448]{1,2,0:T(8,128)} %mul.46, bf16[2,4096,448]{1,2,0:T(8,128)(2,1)} %all-gather.3.cloned.1.call-done), kind=kLoop, calls=%fused_computation.1 | loop fusion | flops 11010048 | bytes 29360128 | tf_op jit(solution)/shard_map/convert_element_type | solution.py:53
  168.8 3.3 %fusion.8 = f32[128,448]{0,1:T(8,128)S(1)} fusion(bf16[128,4096]{0,1:T(8,128)(2,1)S(1)} %bitcast.54, bf16[2,4096,448]{1,2,0:T(8,128)(2,1)} %multiply_convert_fusion), kind=kOutput, calls=%fused_computation.17 | convolution fusion | flops 469762048 | bytes 4947968 | tf_op jit(solution)/shard_map/dot_general | solution.py:67
  172.1 0.9 copy-done
  173.0 1.8 fusion.12
  175.5 2.8 fusion.4
  178.3 2.8 fusion
  181.1 1.3 bitcast_bitcast_fusion
  182.4 11.8 %all-to-all-start.1 = ((bf16[32,128,128]{2,1,0:T(8,128)(2,1)}), bf16[32,128,128]{2,1,0:T(8,128)(2,1)S(1)}, u32[]{:S(2)}, u32[]{:S(2)}) async-start(bf16[32,128,128]{2,1,0:T(8,128)(2,1)} %bitcast_bitcast_fusion), calls=%async_computation.1 | async-start | bytes 2097152 | tf_op jit(solution)/shard_map/all_to_all | solution.py:36
  194.2 1.3 copy.29
  195.6 26.8 %all-to-all-done.1 = bf16[32,128,128]{2,1,0:T(8,128)(2,1)S(1)} async-done(((bf16[32,128,128]{2,1,0:T(8,128)(2,1)}), bf16[32,128,128]{2,1,0:T(8,128)(2,1)S(1)}, u32[]{:S(2)}, u32[]{:S(2)}) %all-to-all-start.1) | async-done | bytes 1048608 | tf_op jit(solution)/shard_map/all_to_all | solution.py:36
  222.3 5.3 %all-to-all-start.2 = ((bf16[128,16,256]{2,0,1:T(8,128)(2,1)}), bf16[128,16,256]{2,0,1:T(8,128)(2,1)S(1)}, u32[]{:S(2)}, u32[]{:S(2)}) async-start(bf16[128,16,256]{2,0,1:T(8,128)(2,1)} %copy.29), calls=%async_computation.2 | async-start | bytes 2097152 | tf_op jit(solution)/shard_map/all_to_all | solution.py:87
  227.6 0.8 reduce_sum.21
  228.4 63.1 %all-gather.5.cloned.1.call-done = bf16[2048,896]{0,1:T(8,128)(2,1)} async-done(((bf16[128,896]{0,1:T(8,128)(2,1)}), bf16[2048,896]{0,1:T(8,128)(2,1)}) %all-gather.5.cloned.1.call-update) | async-done | bytes 3670032 | tf_op jit(solution)/shard_map/all_gather | solution.py:42
  291.5 2.5 slice_bitcast_fusion.7
  294.0 2.2 copy_bitcast_fusion
  296.3 3.6 %convert_reduce_fusion = f32[896,256]{1,0:T(8,128)S(1)} fusion(bf16[16,128,448]{1,2,0:T(8,128)(2,1)S(1)} %get-tuple-element.8, bf16[16,128,448]{1,2,0:T(8,128)(2,1)} %get-tuple-element.9, bf16[128,16,256]{2,0,1:T(8,128)(2,1)S(1)} %all-to-all-done.2), kind=kOutput, calls=%fused_computation | convolution fusion | flops 957644800 | bytes 5636096 | tf_op jit(solution)/shard_map/dot_general | solution.py:95
  299.9 1.0 broadcast_multiply_fusion
  (15 shorter events, 1.7 us)
Async XLA Ops:
  7.2 15.9 %copy-start.1 = (bf16[2,2,448]{2,1,0:T(2,128)(2,1)S(1)}, bf16[2,2,448]{2,1,0:T(2,128)(2,1)}, u32[]{:S(2)}) copy-start(bf16[2,2,448]{2,1,0:T(2,128)(2,1)} %param.6) | copy-start | bytes 10756
  7.2 151.0 %all-gather.3.cloned.1.call-start = ((), (), s32[]{:S(2)}) async-start(), calls=%async_computation.3 | async-start | bytes 7798784 | tf_op jit(solution)/shard_map/all_gather | solution.py:62
  10.1 158.7 %all-to-all-start = ((bf16[32,128,128]{1,2,0:T(8,128)(2,1)}), bf16[32,128,128]{1,2,0:T(8,128)(2,1)S(1)}, u32[]{:S(2)}, u32[]{:S(2)}) async-start(bf16[32,128,128]{1,2,0:T(8,128)(2,1)} %broadcast_in_dim.2), calls=%async_computation | async-start | bytes 2097152 | tf_op jit(solution)/shard_map/all_to_all | solution.py:13
  23.0 268.5 %all-gather.5.cloned.1.call-start = ((), (), s32[]{:S(2)}) async-start(), calls=%async_computation.4 | async-start | bytes 3899392 | tf_op jit(solution)/shard_map/all_gather | solution.py:42
  158.2 13.9 %copy-start.2 = (bf16[128,448]{0,1:T(8,128)(2,1)S(1)}, bf16[128,448]{0,1:T(8,128)(2,1)}, u32[]{:S(2)}) copy-start(bf16[128,448]{0,1:T(8,128)(2,1)} %param.7) | copy-start | bytes 344068
  168.8 4.2 %copy-start = (bf16[2,4096,448]{1,2,0:T(8,128)(2,1)S(1)}, bf16[2,4096,448]{1,2,0:T(8,128)(2,1)}, u32[]{:S(2)}) copy-start(bf16[2,4096,448]{1,2,0:T(8,128)(2,1)} %multiply_convert_fusion) | copy-start | bytes 22020100
  182.4 39.9 %all-to-all-start.1 = ((bf16[32,128,128]{2,1,0:T(8,128)(2,1)}), bf16[32,128,128]{2,1,0:T(8,128)(2,1)S(1)}, u32[]{:S(2)}, u32[]{:S(2)}) async-start(bf16[32,128,128]{2,1,0:T(8,128)(2,1)} %bitcast_bitcast_fusion), calls=%async_computation.1 | async-start | bytes 2097152 | tf_op jit(solution)/shard_map/all_to_all | solution.py:36
  222.3 74.0 %all-to-all-start.2 = ((bf16[128,16,256]{2,0,1:T(8,128)(2,1)}), bf16[128,16,256]{2,0,1:T(8,128)(2,1)S(1)}, u32[]{:S(2)}, u32[]{:S(2)}) async-start(bf16[128,16,256]{2,0,1:T(8,128)(2,1)} %copy.29), calls=%async_computation.2 | async-start | bytes 2097152 | tf_op jit(solution)/shard_map/all_to_all | solution.py:87
Sparse Core Ops, SparseCore 0:
  11.0 147.0 all-gather.2
  175.6 115.8 all-gather.4
where the time goes:
time: 312 us; the launch traced here: 308 us
  waiting for transfers between devices  166 us (53%)
  blocking collectives  35.1 us (11%)
  local copies, waits for them, and re-layouts  34.5 us (11%)
  starting transfers between devices  30.1 us (10%)
  matrix products  14.3 us (5%)
  between operations  14.1 us (5%)
  other arithmetic  13.1 us (4%)
    all_gather x1, waiting for transfers between devices, body(): lax.all_gather(gate_up_codes, 'local', axis=1, tiled=True)  75.9 us
    all_gather x1, waiting for transfers between devices, sent_together(): out, at, outs = (lax.all_gather(both, axis, axis=dim, tiled=True), 0, [])  63.1 us
    all_gather x1, blocking collectives, body(): lax.all_gather(gate_up_scales, 'local', axis=1, tiled=True)  35.1 us
    all_to_all x1, waiting for transfers between devices, sent_and_summed(): lax.all_to_all(pieces, axis, split_axis=0, concat_axis=0, tiled=True)  26.8 us
    mul x2, local copies, waits for them, and re-layouts, dequant(): weight = blocked * scales.astype(jnp.float32)[..., :, None, :]  23.9 us
    all_to_all x1, starting transfers between devices, from_everyone(): lax.all_to_all(jnp.broadcast_to(array[None], (length, *array.shape)), axi...  12.9 us
    all_to_all x1, starting transfers between devices, sent_and_summed(): lax.all_to_all(pieces, axis, split_axis=0, concat_axis=0, tiled=True)  11.8 us
    convert_element_type x1, other arithmetic, dequant(): return weight.reshape(shape).astype(jnp.bfloat16)  10.6 us
  transfers between devices with their start and end apart: 5, of which 3 were waited for; matrix products, arithmetic and copies ran while one was open for 16% of the time, Pallas kernels for 0%

commit v1 on v0

v1 whole, which is shorter than its diff:
```python
import math

import jax
import jax.numpy as jnp
from jax import lax
from jax.experimental import pallas as pl
from jax.experimental.pallas import tpu as pltpu
from jax.sharding import PartitionSpec as P

MESH = pl.DeviceIdType.MESH
BLOCK = 128
NY = 8
NZ = 8
CHUNKS = 4
F32 = jnp.float32
BF16 = jnp.bfloat16


def dot_nn(a, b):
    return lax.dot_general(a, b, (((1,), (0,)), ((), ())), preferred_element_type=F32)


def dot_nt(a, b):
    return lax.dot_general(a, b, (((1,), (1,)), ((), ())), preferred_element_type=F32)


def kernel(
    tok_ref,
    codes_ref,
    scale_ref,
    dh_ref,
    hid_ref,
    dtok_ref,
    grad_ref,
    xin,
    x,
    w,
    wt,
    rs0,
    rs,
    part,
    own,
    dg,
    acc,
    dp,
    sib,
    zin,
    zsum,
    dtin,
    gsend,
    grecv,
    loc_sem,
    w_s,
    w_r,
    xg_s,
    xg_r,
    xp_s,
    xp_r,
    xm_s,
    xm_r,
    xs_s,
    xs_r,
    rs_s,
    rs_r,
    ag_s,
    ag_r,
    sb_s,
    sb_r,
    zl_s,
    zl_r,
    zs_s,
    zs_r,
    dt_s,
    dt_r,
    g_s,
    g_r,
):
    n = lax.axis_index("node")
    l = lax.axis_index("local")
    z = lax.div(n, 4)
    xl = lax.rem(lax.div(n, 2), 2)
    c = lax.rem(n, 2)
    h = lax.div(l, NY)
    y = lax.rem(l, NY)
    half = codes_ref.shape[1] // CHUNKS
    rows = 2 * half

    def dev(z_, xl_, c_, h_, y_):
        return (z_ * 4 + xl_ * 2 + c_, h_ * NY + y_)

    zu = lax.rem(z + 1, NZ)
    zd = lax.rem(z + NZ - 1, NZ)
    yu = lax.rem(y + 1, NY)
    yd = lax.rem(y + NY - 1, NY)
    up_z = dev(zu, xl, c, h, y)
    dn_z = dev(zd, xl, c, h, y)
    up_y = dev(z, xl, c, h, yu)
    dn_y = dev(z, xl, c, h, yd)
    sibling = dev(z, xl, 1 - c, h, y)
    partner = dev(z, xl, c, 1 - h, y)
    other = 1 - c

    barrier = pltpu.get_barrier_semaphore()
    peers = [up_z, dn_z, sibling, partner]
    for dx in range(2):
        for dy in range(NY):
            if dx or dy:
                peers.append(dev(z, lax.rem(xl + dx, 2), c, h, lax.rem(y + dy, NY)))
    for peer in peers:
        pl.semaphore_signal(barrier, inc=1, device_id=peer, device_id_type=MESH)

    def remote(src, dst, ss, rr, to):
        return pltpu.make_async_remote_copy(
            src_ref=src, dst_ref=dst, send_sem=ss, recv_sem=rr, device_id=to, device_id_type=MESH
        )

    for k in range(2):
        for i in range(CHUNKS):
            f = pl.ds(half * i, half)
            code = codes_ref[k, f, :].astype(F32)
            sc = scale_ref[k, f, :]
            s = jnp.concatenate(
                [jnp.broadcast_to(sc[:, b : b + 1], (half, BLOCK)) for b in range(2)], axis=1
            )
            w[h, pl.ds(rows * i + half * k, half), :] = (code * s).astype(BF16)
    xin[...] = tok_ref[...]

    pl.semaphore_wait(barrier, len(peers))

    wcopy = remote(w.at[h], w.at[h], w_s, w_r, partner)
    wcopy.start()

    ystar = 2 * lax.rem(z, 4) + xl
    qsrc = lax.div(z, 4)
    myslot = x.at[2 * qsrc + c, y]
    own_col = dev(z, xl, c, h, ystar)
    oth_col = dev(z, 1 - xl, c, h, ystar)
    xg0 = remote(xin, myslot, xg_s.at[0], xg_r.at[y], own_col)
    xg1 = remote(xin, myslot, xg_s.at[1], xg_r.at[y], oth_col)
    xg1.start()
    selfcol = ystar == y

    @pl.when(selfcol)
    def _():
        pltpu.make_async_copy(xin, myslot, xg_r.at[y]).start()

    @pl.when(jnp.logical_not(selfcol))
    def _():
        xg0.start()

    dz = lax.rem(z - lax.div(y, 2) + NZ, NZ)
    r = lax.rem(dz, 4)
    qo = lax.div(dz, 4)
    qp = lax.div(lax.rem(dz + 7, NZ), 4)
    qm = 1 - qp

    def block(d):
        return lax.rem(y + d + NY, NY)

    order = [block(d) for d in (4, 3, -3, 2, -2, 1, -1, 0)]

    def slot(q, tb):
        return x.at[2 * q + c, tb]

    def cp_plus(q, i):
        s = slot(q, order[i])
        return remote(s, s, xp_s.at[i], xp_r.at[i], up_z)

    def cp_minus(q, i):
        s = slot(q, order[i])
        return remote(s, s, xm_s.at[i], xm_r.at[i], dn_z)

    def cp_sib(q, i):
        s = slot(q, order[i])
        return remote(s, s, xs_s.at[q, i], xs_r.at[q, i], sibling)

    @pl.when(r == 0)
    def _():
        for i in range(NY):
            s = slot(qo, order[i])
            remote(xin, s, xg_s.at[0], xg_r.at[order[i]], own_col).wait_recv()
            cp_plus(qo, i).start()
            cp_minus(qo, i).start()
            cp_sib(qo, i).start()
        for i in range(NY):
            cp_plus(qp, i).wait_recv()
            cp_sib(qp, i).start()

    @pl.when(r == 1)
    def _():
        for i in range(NY):
            cp_plus(qp, i).wait_recv()
            cp_plus(qp, i).start()
            cp_sib(qp, i).start()
        for i in range(NY):
            cp_minus(qm, i).wait_recv()
            cp_sib(qm, i).start()

    @pl.when(r == 2)
    def _():
        for i in range(NY):
            cp_plus(qp, i).wait_recv()
            cp_plus(qp, i).start()
            cp_sib(qp, i).start()
            cp_minus(qm, i).wait_recv()
            cp_minus(qm, i).start()
            cp_sib(qm, i).start()

    @pl.when(r == 3)
    def _():
        for i in range(NY):
            cp_minus(qm, i).wait_recv()
            cp_minus(qm, i).start()
            cp_sib(qm, i).start()
        for i in range(NY):
            cp_plus(qp, i).wait_recv()
            cp_plus(qp, i).start()
            cp_sib(qp, i).start()

    for q in range(2):
        for i in range(NY):
            s = x.at[2 * q + other, order[i]]
            remote(s, s, xs_s.at[q, i], xs_r.at[q, i], sibling).wait_recv()

    remote(w.at[1 - h], w.at[1 - h], w_s, w_r, partner).wait_recv()

    def xq(q, tb):
        return jnp.concatenate([x[2 * q, tb], x[2 * q + 1, tb]], axis=1)

    def partial(tb, lo, hi):
        a = slice(lo * rows, hi * rows)
        return dot_nt(w[0, a, :], xq(0, tb)) + dot_nt(w[1, a, :], xq(1, tb))

    def ch(i):
        return pl.ds(rows * i, rows)

    nbr = (up_y, dn_y)
    hc = CHUNKS // 2

    def rs_copy(s, d, i):
        src = rs0.at[d, ch(i - hc * d)] if s == 0 else rs.at[d, s - 1, ch(i)]
        return remote(src, rs.at[d, s, ch(i)], rs_s.at[s, d, i], rs_r.at[s, d, i], nbr[d])

    def firsts(d):
        return range(hc) if d == 0 else range(hc, CHUNKS)

    p0 = partial(block(4), 0, CHUNKS)
    for d in range(2):
        rs0[d] = p0[d * hc * rows : (d + 1) * hc * rows].astype(BF16)
        for i in firsts(d):
            rs_copy(0, d, i).start()
    for s in range(1, 4):
        for d in range(2):
            part[d] = partial(block(4 - s if d == 0 else s - 4), 0, CHUNKS)
        if s == 1:
            for d in range(2):
                for i in firsts(1 - d):
                    rs[d, 0, ch(i)] = part[d, ch(i)].astype(BF16)
                    rs_copy(1, d, i).start()
        for i in range(CHUNKS):
            for d in range(2):
                if s == 1:
                    if i not in firsts(d):
                        continue
                rs_copy(s - 1, d, i).wait_recv()
                rs[d, s - 1, ch(i)] = (rs[d, s - 1, ch(i)].astype(F32) + part[d, ch(i)]).astype(BF16)
                rs_copy(s, d, i).start()
    own[...] = partial(y, 0, CHUNKS)

    def ag_copy(s, d, i):
        b = lax.rem(y + (NY - s if d == 0 else s), NY)
        sl = dg.at[b, ch(i)]
        return remote(sl, sl, ag_s.at[s, d, i], ag_r.at[s, d, i], nbr[d])

    def ag_wait(s, d, i):
        b = lax.rem(y + (NY - 1 - s if d == 0 else s + 1), NY)
        sl = dg.at[b, ch(i)]
        remote(sl, sl, ag_s.at[s, d, i], ag_r.at[s, d, i], nbr[d]).wait_recv()

    for i in range(CHUNKS):
        for d in range(2):
            rs_copy(3, d, i).wait_recv()
        tot = own[ch(i)] + rs[0, 3, ch(i)].astype(F32) + rs[1, 3, ch(i)].astype(F32)
        gate, up = tot[:half], tot[half:]
        f = pl.ds(half * i, half)
        sg = jax.nn.sigmoid(gate)
        act = gate * sg
        hid_ref[f, :] = (act * up).astype(BF16)
        gin = dh_ref[f, :].astype(F32)
        dgate = (gin * up * sg * (1.0 + gate * (1.0 - sg))).astype(BF16)
        dup = (gin * act).astype(BF16)
        dg[y, pl.ds(rows * i, half), :] = dgate
        dg[y, pl.ds(rows * i + half, half), :] = dup
        for d in range(2):
            ag_copy(0, d, i).start()

    for q in range(2):
        wt[q] = jnp.transpose(w[q])

    def grads_of(blocks, first):
        a = jnp.concatenate([dg[b] for b in blocks], axis=1) if len(blocks) > 1 else dg[blocks[0]]
        for j in range(4):
            xs = [x[j, b] for b in blocks]
            bb = jnp.concatenate(xs, axis=0) if len(blocks) > 1 else xs[0]
            v = dot_nn(a, bb)
            col = slice(128 * (j % 2), 128 * (j % 2) + 128)
            if first:
                acc[j // 2, :, col] = v
            else:
                acc[j // 2, :, col] = acc[j // 2, :, col] + v

    def sib_copy(q, b, k):
        return remote(
            dp.at[2 * q + other, b], sib.at[q, k], sb_s.at[q, k], sb_r.at[q, k], sibling
        )

    def inputs_of(b, k):
        for q in range(2):
            v = dot_nn(wt[q], dg[b]).astype(BF16)
            dp[2 * q, b] = v[:128]
            dp[2 * q + 1, b] = v[128:]
            sib_copy(q, b, k).start()

    seq = [block(d) for d in (0, -1, 1, -2, 2, -3, 3, 4)]
    inputs_of(seq[0], 0)
    grads_of([seq[0]], True)
    for s in range(1, 5):
        for i in range(CHUNKS):
            for d in range(2):
                if s < 4 or i in firsts(d):
                    ag_wait(s - 1, d, i)
                if s < 3 or (s == 3 and i in firsts(d)):
                    ag_copy(s, d, i).start()
        if s < 4:
            inputs_of(seq[2 * s - 1], 2 * s - 1)
            inputs_of(seq[2 * s], 2 * s)
            grads_of([seq[2 * s - 1], seq[2 * s]], False)
        else:
            inputs_of(seq[7], 7)
            grads_of([seq[7]], False)

    gsend[...] = acc[1 - h].astype(BF16)
    gcopy = remote(gsend, grecv, g_s, g_r, partner)
    gcopy.start()

    for k in range(NY):
        for q in range(2):
            sib_copy(q, seq[k], k).wait_recv()
            v = dp[2 * q + c, seq[k]].astype(F32) + sib[q, k].astype(F32)
            zsum[q, k] = v.astype(BF16)

    def z_long(q, k):
        return remote(zsum.at[q, k], zin.at[0, k], zl_s.at[k], zl_r.at[k], dn_z)

    def z_short(q, k):
        return remote(zsum.at[q, k], zin.at[1, k], zs_s.at[k], zs_r.at[k], up_z)

    def long_hop(k):
        z_long(qp, k).wait_recv()
        zsum[qp, k] = (zsum[qp, k].astype(F32) + zin[0, k].astype(F32)).astype(BF16)
        z_long(qp, k).start()

    def short_hop(k):
        z_short(qm, k).wait_recv()
        zsum[qm, k] = (zsum[qm, k].astype(F32) + zin[1, k].astype(F32)).astype(BF16)
        z_short(qm, k).start()

    par = lax.rem(y, 2)

    @pl.when(r == 1)
    def _():
        for k in range(NY):
            z_short(qm, k).start()
        for k in range(NY):
            long_hop(k)

    @pl.when(r == 2)
    def _():
        for k in range(NY):
            short_hop(k)
            long_hop(k)

    @pl.when(r == 3)
    def _():
        for k in range(NY):
            long_hop(k)
        for k in range(NY):
            short_hop(k)

    def dt_copy(k, tb):
        return remote(
            zsum.at[qo, k], dtin.at[xl], dt_s.at[k], dt_r.at[xl], dev(z, par, c, h, tb)
        )

    mine = jnp.logical_and(r == 0, xl == par)

    @pl.when(r == 0)
    def _():
        for k in range(NY):
            z_long(qp, k).start()
        for k in range(NY):
            z_long(qp, k).wait_recv()
            z_short(qm, k).wait_recv()
            zsum[qo, k] = (
                zsum[qo, k].astype(F32) + zin[0, k].astype(F32) + zin[1, k].astype(F32)
            ).astype(BF16)
            if k > 0:
                dt_copy(k, seq[k]).start()
            else:

                @pl.when(xl == par)
                def _():
                    pltpu.make_async_copy(zsum.at[qo, 0], dtin.at[xl], dt_r.at[xl]).start()

                @pl.when(xl != par)
                def _():
                    dt_copy(0, seq[0]).start()

    remote(gsend, grecv, g_s, g_r, partner).wait_recv()
    for i in range(CHUNKS):
        for k in range(2):
            a = pl.ds(rows * i + half * k, half)
            grad_ref[k, pl.ds(half * i, half), :] = acc[h, a, :] + grecv[a, :].astype(F32)

    for s in range(2):
        remote(zsum.at[0, 0], dtin.at[s], dt_s.at[0], dt_r.at[s], sibling).wait_recv()
    tot = dtin[0].astype(F32) + dtin[1].astype(F32)
    dtok_ref[...] = jnp.transpose(tot).astype(BF16)

    wcopy.wait_send()
    xg1.wait_send()

    @pl.when(jnp.logical_not(selfcol))
    def _():
        xg0.wait_send()

    for i in range(NY):
        cp_plus(0, i).wait_send()
        for q in range(2):
            cp_sib(q, i).wait_send()

    @pl.when(r != 1)
    def _():
        for i in range(NY):
            cp_minus(0, i).wait_send()

    for s in range(4):
        for d in range(2):
            for i in range(CHUNKS):
                if s > 0 or i in firsts(d):
                    rs_copy(s, d, i).wait_send()
                if s < 3 or i in firsts(d):
                    ag_copy(s, d, i).wait_send()
    for k in range(NY):
        for q in range(2):
            sib_copy(q, seq[k], k).wait_send()
        z_long(0, k).wait_send()

    @pl.when(r != 0)
    def _():
        for k in range(NY):
            z_short(0, k).wait_send()

    @pl.when(r == 0)
    def _():
        for k in range(1, NY):
            dt_copy(k, seq[k]).wait_send()

    @pl.when(jnp.logical_and(r == 0, xl != par))
    def _():
        dt_copy(0, seq[0]).wait_send()

    gcopy.wait_send()


def body(tokens, codes, scales, d_hidden):
    t, dloc = tokens.shape
    _, wrows, group = codes.shape
    all2 = 2 * group
    codes_t = jnp.transpose(codes, (0, 2, 1))
    scale_t = jnp.transpose(scales, (0, 2, 1)).astype(F32)
    dh_t = jnp.transpose(d_hidden)
    dma = pltpu.SemaphoreType.DMA
    vm = pl.BlockSpec(memory_space=pltpu.VMEM)
    hid_t, dtok, grad_t = pl.pallas_call(
        kernel,
        out_shape=(
            jax.ShapeDtypeStruct((group, t), BF16),
            jax.ShapeDtypeStruct((t, dloc), BF16),
            jax.ShapeDtypeStruct((2, group, wrows), F32),
        ),
        in_specs=[vm] * 4,
        out_specs=(vm, vm, vm),
        scratch_shapes=[
            pltpu.VMEM((t, dloc), BF16),
            pltpu.VMEM((4, NY, t, dloc), BF16),
            pltpu.VMEM((2, all2, wrows), BF16),
            pltpu.VMEM((2, wrows, all2), BF16),
            pltpu.VMEM((2, all2 // 2, t), BF16),
            pltpu.VMEM((2, 4, all2, t), BF16),
            pltpu.VMEM((2, all2, t), F32),
            pltpu.VMEM((all2, t), F32),
            pltpu.VMEM((NY, all2, t), BF16),
            pltpu.VMEM((2, all2, wrows), F32),
            pltpu.VMEM((4, NY, dloc, t), BF16),
            pltpu.VMEM((2, NY, dloc, t), BF16),
            pltpu.VMEM((2, NY, dloc, t), BF16),
            pltpu.VMEM((2, NY, dloc, t), BF16),
            pltpu.VMEM((2, dloc, t), BF16),
            pltpu.VMEM((all2, wrows), BF16),
            pltpu.VMEM((all2, wrows), BF16),
            dma(()),
            dma(()),
            dma(()),
            dma((2,)),
            dma((NY,)),
            dma((NY,)),
            dma((NY,)),
            dma((NY,)),
            dma((NY,)),
            dma((2, NY)),
            dma((2, NY)),
            dma((4, 2, CHUNKS)),
            dma((4, 2, CHUNKS)),
            dma((4, 2, CHUNKS)),
            dma((4, 2, CHUNKS)),
            dma((2, NY)),
            dma((2, NY)),
            dma((NY,)),
            dma((NY,)),
            dma((NY,)),
            dma((NY,)),
            dma((NY,)),
            dma((2,)),
            dma(()),
            dma(()),
        ],
        compiler_params=pltpu.CompilerParams(collective_id=0, has_side_effects=True),
    )(tokens, codes_t, scale_t, dh_t)
    factor = 1.0 / math.sqrt(t * lax.axis_size("local"))
    return (jnp.transpose(hid_t), dtok, jnp.transpose(grad_t, (0, 2, 1)) * factor)


def solution(mesh):
    return jax.shard_map(
        body,
        mesh=mesh,
        in_specs=(
            P("local", "node"),
            P(None, "local", "node"),
            P(None, "local", "node"),
            P("local", "node"),
        ),
        out_specs=(P("local", "node"), P("local", "node"), P(None, "local", "node")),
        check_vma=False,
    )
```

time: 312 us -> 114 us (0.37)
  the two profiles are of different devices: /device:TPU:1 before, /device:TPU:126 now
where the time goes in v1:
time: 114 us
  Pallas kernels  108 us (95%)
  local copies, waits for them, and re-layouts  3 us (3%)
  other arithmetic  2.22 us (2%)
    pallas_call x1, Pallas kernels, body(): pl.pallas_call(kernel, out_shape=(jax.ShapeDtypeStruct((group, t), BF16),...  108 us

profile of v1, /device:TPU:126, one launch (start us, length us, event | category | flops | bytes accessed | tf_op | source)
XLA Modules:
  0.0 113.9 jit_solution(16608924149662835235)
XLA Ops:
  0.6 1.6 %copy.7 = f32[2,2,448]{1,2,0:T(8,128)} copy(bf16[2,2,448]{2,1,0:T(2,128)(2,1)} %param.6) | data formatting | bytes 10752 | tf_op jit(solution)/shard_map/convert_element_type | solution.py:481
  2.3 108.0 %shard_map.67 = (bf16[448,128]{1,0:T(8,128)(2,1)}, bf16[128,128]{1,0:T(8,128)(2,1)}, f32[2,448,256]{2,1,0:T(8,128)}) custom-call(bf16[128,128]{1,0:T(8,128)(2,1)} %tok_ref.1, bf16[2,448,256]{2,1,0:T(8,128)(2,1)} %bitcast.7, f32[2,448,2]{2,1,0:T(8,128)} %bitcast.6, bf16[448,128]{1,0:T(8,128)(2,1)} %bitcast.8), custom_call_target="tpu_custom_call" | custom-call | tf_op jit(solution)/shard_map/pallas_call | solution.py:485
  110.3 0.0 copy-start
  110.3 2.2 %multiply_bitcast_fusion = f32[2,256,448]{1,2,0:T(8,128)} fusion(f32[2,448,256]{2,1,0:T(8,128)} %get-tuple-element.8), kind=kLoop, calls=%fused_computation | loop fusion | flops 229376 | bytes 1835008 | tf_op jit(solution)/shard_map/mul | solution.py:541
  112.5 0.0 copy-done
  112.5 0.0 copy-start.1
  112.5 0.6 copy.10
  113.1 0.1 copy-done.1
  113.3 0.6 copy.11
Async XLA Ops:
  110.3 2.2 %copy-start = (bf16[448,128]{1,0:T(8,128)(2,1)S(1)}, bf16[448,128]{1,0:T(8,128)(2,1)}, u32[]{:S(2)}) copy-start(bf16[448,128]{1,0:T(8,128)(2,1)} %get-tuple-element.6) | copy-start | bytes 344068
  112.5 0.8 copy-start.1

commit v2 on v1

--- a/solution.py
+++ b/solution.py
@@ -25,13 +25,17 @@
 
 
 def kernel(
-    tok_ref,
+    tok_hbm,
+    codes_hbm,
+    scale_hbm,
+    dh_hbm,
+    hid_ref,
+    dtok_ref,
+    grad_ref,
     codes_ref,
     scale_ref,
     dh_ref,
-    hid_ref,
-    dtok_ref,
-    grad_ref,
+    in_sem,
     xin,
     x,
     w,
@@ -66,15 +70,22 @@
     ag_r,
     sb_s,
     sb_r,
-    zl_s,
-    zl_r,
-    zs_s,
-    zs_r,
+    zo_s,
+    zo_r,
     dt_s,
     dt_r,
     g_s,
     g_r,
 ):
+    loads = [
+        pltpu.make_async_copy(a, b, in_sem.at[i])
+        for i, (a, b) in enumerate(
+            ((tok_hbm, xin), (scale_hbm, scale_ref), (codes_hbm, codes_ref), (dh_hbm, dh_ref))
+        )
+    ]
+    for load in loads:
+        load.start()
+
     n = lax.axis_index("node")
     l = lax.axis_index("local")
     z = lax.div(n, 4)
@@ -83,6 +94,7 @@
     h = lax.div(l, NY)
     y = lax.rem(l, NY)
     half = codes_ref.shape[1] // CHUNKS
+    factor = 1.0 / math.sqrt(tok_hbm.shape[0] * 16)
     rows = 2 * half
 
     def dev(z_, xl_, c_, h_, y_):
@@ -92,7 +104,11 @@
     zd = lax.rem(z + NZ - 1, NZ)
     yu = lax.rem(y + 1, NY)
     yd = lax.rem(y + NY - 1, NY)
+    zu2 = lax.rem(z + 2, NZ)
+    zd2 = lax.rem(z + NZ - 2, NZ)
     up_z = dev(zu, xl, c, h, y)
+    up_z2 = dev(zu2, xl, c, h, y)
+    dn_z2 = dev(zd2, xl, c, h, y)
     dn_z = dev(zd, xl, c, h, y)
     up_y = dev(z, xl, c, h, yu)
     dn_y = dev(z, xl, c, h, yd)
@@ -101,7 +117,7 @@
     other = 1 - c
 
     barrier = pltpu.get_barrier_semaphore()
-    peers = [up_z, dn_z, sibling, partner]
+    peers = [up_z, dn_z, up_z2, dn_z2, sibling, partner]
     for dx in range(2):
         for dy in range(NY):
             if dx or dy:
@@ -114,16 +130,27 @@
             src_ref=src, dst_ref=dst, send_sem=ss, recv_sem=rr, device_id=to, device_id_type=MESH
         )
 
+    loads[1].wait()
+    loads[2].wait()
+    pick = (
+        lax.broadcasted_iota(jnp.int32, (2, 2 * BLOCK), 1) // BLOCK
+        == lax.broadcasted_iota(jnp.int32, (2, 2 * BLOCK), 0)
+    ).astype(F32)
     for k in range(2):
+        spread = lax.dot_general(
+            scale_ref[k].astype(F32),
+            pick,
+            (((0,), (0,)), ((), ())),
+            precision=lax.Precision.HIGHEST,
+            preferred_element_type=F32,
+        )
         for i in range(CHUNKS):
             f = pl.ds(half * i, half)
             code = codes_ref[k, f, :].astype(F32)
-            sc = scale_ref[k, f, :]
-            s = jnp.concatenate(
-                [jnp.broadcast_to(sc[:, b : b + 1], (half, BLOCK)) for b in range(2)], axis=1
-            )
+            s = spread[half * i : half * (i + 1)]
             w[h, pl.ds(rows * i + half * k, half), :] = (code * s).astype(BF16)
-    xin[...] = tok_ref[...]
+    loads[0].wait()
+    loads[3].wait()
 
     pl.semaphore_wait(barrier, len(peers))
 
@@ -162,66 +189,82 @@
     def slot(q, tb):
         return x.at[2 * q + c, tb]
 
-    def cp_plus(q, i):
+    def cp_plus(q, i, far):
         s = slot(q, order[i])
-        return remote(s, s, xp_s.at[i], xp_r.at[i], up_z)
-
-    def cp_minus(q, i):
+        return remote(s, s, xp_s.at[far, i], xp_r.at[i], up_z2 if far else up_z)
+
+    def cp_minus(q, i, far):
         s = slot(q, order[i])
-        return remote(s, s, xm_s.at[i], xm_r.at[i], dn_z)
+        return remote(s, s, xm_s.at[far, i], xm_r.at[i], dn_z2 if far else dn_z)
 
     def cp_sib(q, i):
         s = slot(q, order[i])
         return remote(s, s, xs_s.at[q, i], xs_r.at[q, i], sibling)
 
-    @pl.when(r == 0)
-    def _():
-        for i in range(NY):
-            s = slot(qo, order[i])
-            remote(xin, s, xg_s.at[0], xg_r.at[order[i]], own_col).wait_recv()
-            cp_plus(qo, i).start()
-            cp_minus(qo, i).start()
-            cp_sib(qo, i).start()
-        for i in range(NY):
-            cp_plus(qp, i).wait_recv()
-            cp_sib(qp, i).start()
-
-    @pl.when(r == 1)
-    def _():
-        for i in range(NY):
-            cp_plus(qp, i).wait_recv()
-            cp_plus(qp, i).start()
-            cp_sib(qp, i).start()
-        for i in range(NY):
-            cp_minus(qm, i).wait_recv()
-            cp_sib(qm, i).start()
-
-    @pl.when(r == 2)
-    def _():
-        for i in range(NY):
-            cp_plus(qp, i).wait_recv()
-            cp_plus(qp, i).start()
-            cp_sib(qp, i).start()
-            cp_minus(qm, i).wait_recv()
-            cp_minus(qm, i).start()
-            cp_sib(qm, i).start()
-
-    @pl.when(r == 3)
-    def _():
-        for i in range(NY):
-            cp_minus(qm, i).wait_recv()
-            cp_minus(qm, i).start()
-            cp_sib(qm, i).start()
-        for i in range(NY):
-            cp_plus(qp, i).wait_recv()
-            cp_plus(qp, i).start()
-            cp_sib(qp, i).start()
-
-    for q in range(2):
-        for i in range(NY):
+    def sib_wait(i):
+        for q in range(2):
             s = x.at[2 * q + other, order[i]]
             remote(s, s, xs_s.at[q, i], xs_r.at[q, i], sibling).wait_recv()
 
+    def spread_own(i):
+        remote(xin, slot(qo, order[i]), xg_s.at[0], xg_r.at[order[i]], own_col).wait_recv()
+        for far in (1, 0):
+            cp_plus(qo, i, far).start()
+            cp_minus(qo, i, far).start()
+        cp_sib(qo, i).start()
+
+    def take_plus(i):
+        cp_plus(qp, i, 0).wait_recv()
+        cp_sib(qp, i).start()
+
+    def take_minus(i):
+        cp_minus(qm, i, 0).wait_recv()
+        cp_sib(qm, i).start()
+
+    def relay(i):
+        cp_plus(qp, i, 0).wait_recv()
+        cp_plus(qp, i, 1).start()
+        cp_plus(qp, i, 0).start()
+        cp_sib(qp, i).start()
+        cp_minus(qm, i, 0).wait_recv()
+        cp_minus(qm, i, 0).start()
+        cp_sib(qm, i).start()
+
+    stages = ((0,), (1, 2), (3, 4), (5, 6, 7))
+    early = ((0, 1, 2), (3, 4), (5, 6), (7,))
+
+    def tokens_stage(t):
+        @pl.when(r == 0)
+        def _():
+            if t == 0:
+                for i in range(NY):
+                    spread_own(i)
+            for i in stages[t]:
+                take_plus(i)
+
+        @pl.when(r == 1)
+        def _():
+            for i in early[t]:
+                take_plus(i)
+            for i in stages[t]:
+                take_minus(i)
+
+        @pl.when(r == 2)
+        def _():
+            for i in stages[t]:
+                relay(i)
+
+        @pl.when(r == 3)
+        def _():
+            for i in early[t]:
+                take_minus(i)
+            for i in stages[t]:
+                take_plus(i)
+
+        for i in stages[t]:
+            sib_wait(i)
+
+    tokens_stage(0)
     remote(w.at[1 - h], w.at[1 - h], w_s, w_r, partner).wait_recv()
 
     def xq(q, tb):
@@ -250,6 +293,7 @@
         for i in firsts(d):
             rs_copy(0, d, i).start()
     for s in range(1, 4):
+        tokens_stage(s)
         for d in range(2):
             part[d] = partial(block(4 - s if d == 0 else s - 4), 0, CHUNKS)
         if s == 1:
@@ -322,6 +366,68 @@
             sib_copy(q, b, k).start()
 
     seq = [block(d) for d in (0, -1, 1, -2, 2, -3, 3, 4)]
+    groups = ((0,), (1, 2), (3, 4), (5, 6), (7,))
+    par = lax.rem(y, 2)
+
+    z_to = (dn_z, up_z, dn_z2, up_z2)
+
+    def z_copy(q, w_, k):
+        return remote(zsum.at[q, k], zin.at[w_, k], zo_s.at[w_, k], zo_r.at[w_, k], z_to[w_])
+
+    def z_add(q, ways, k):
+        v = zsum[q, k].astype(F32)
+        for w_ in ways:
+            z_copy(q, w_, k).wait_recv()
+            v = v + zin[w_, k].astype(F32)
+        zsum[q, k] = v.astype(BF16)
+
+    def dt_copy(k):
+        return remote(
+            zsum.at[qo, k], dtin.at[xl], dt_s.at[k], dt_r.at[xl], dev(z, par, c, h, seq[k])
+        )
+
+    def cores(g):
+        for k in groups[g]:
+            for q in range(2):
+                sib_copy(q, seq[k], k).wait_recv()
+                v = dp[2 * q + c, seq[k]].astype(F32) + sib[q, k].astype(F32)
+                zsum[q, k] = v.astype(BF16)
+
+            @pl.when(lax.rem(r, 2) == 1)
+            def _():
+                z_copy(qp, 0, k).start()
+                z_copy(qm, 1, k).start()
+
+            @pl.when(r == 0)
+            def _():
+                z_copy(qp, 2, k).start()
+
+    def middle(g):
+        @pl.when(r == 2)
+        def _():
+            for k in groups[g]:
+                z_add(qp, (0, 2), k)
+                z_copy(qp, 2, k).start()
+                z_add(qm, (1,), k)
+                z_copy(qm, 3, k).start()
+
+    def collect(g):
+        @pl.when(r == 0)
+        def _():
+            for k in groups[g]:
+                z_add(qo, (0, 1, 2, 3), k)
+                if k > 0:
+                    dt_copy(k).start()
+                else:
+
+                    @pl.when(xl == par)
+                    def _():
+                        pltpu.make_async_copy(zsum.at[qo, 0], dtin.at[xl], dt_r.at[xl]).start()
+
+                    @pl.when(xl != par)
+                    def _():
+                        dt_copy(0).start()
+
     inputs_of(seq[0], 0)
     grads_of([seq[0]], True)
     for s in range(1, 5):
@@ -331,96 +437,32 @@
                     ag_wait(s - 1, d, i)
                 if s < 3 or (s == 3 and i in firsts(d)):
                     ag_copy(s, d, i).start()
-        if s < 4:
-            inputs_of(seq[2 * s - 1], 2 * s - 1)
-            inputs_of(seq[2 * s], 2 * s)
-            grads_of([seq[2 * s - 1], seq[2 * s]], False)
-        else:
-            inputs_of(seq[7], 7)
-            grads_of([seq[7]], False)
-
-    gsend[...] = acc[1 - h].astype(BF16)
-    gcopy = remote(gsend, grecv, g_s, g_r, partner)
-    gcopy.start()
-
-    for k in range(NY):
-        for q in range(2):
-            sib_copy(q, seq[k], k).wait_recv()
-            v = dp[2 * q + c, seq[k]].astype(F32) + sib[q, k].astype(F32)
-            zsum[q, k] = v.astype(BF16)
-
-    def z_long(q, k):
-        return remote(zsum.at[q, k], zin.at[0, k], zl_s.at[k], zl_r.at[k], dn_z)
-
-    def z_short(q, k):
-        return remote(zsum.at[q, k], zin.at[1, k], zs_s.at[k], zs_r.at[k], up_z)
-
-    def long_hop(k):
-        z_long(qp, k).wait_recv()
-        zsum[qp, k] = (zsum[qp, k].astype(F32) + zin[0, k].astype(F32)).astype(BF16)
-        z_long(qp, k).start()
-
-    def short_hop(k):
-        z_short(qm, k).wait_recv()
-        zsum[qm, k] = (zsum[qm, k].astype(F32) + zin[1, k].astype(F32)).astype(BF16)
-        z_short(qm, k).start()
-
-    par = lax.rem(y, 2)
-
-    @pl.when(r == 1)
-    def _():
-        for k in range(NY):
-            z_short(qm, k).start()
-        for k in range(NY):
-            long_hop(k)
-
-    @pl.when(r == 2)
-    def _():
-        for k in range(NY):
-            short_hop(k)
-            long_hop(k)
-
-    @pl.when(r == 3)
-    def _():
-        for k in range(NY):
-            long_hop(k)
-        for k in range(NY):
-            short_hop(k)
-
-    def dt_copy(k, tb):
-        return remote(
-            zsum.at[qo, k], dtin.at[xl], dt_s.at[k], dt_r.at[xl], dev(z, par, c, h, tb)
-        )
-
-    mine = jnp.logical_and(r == 0, xl == par)
-
-    @pl.when(r == 0)
-    def _():
-        for k in range(NY):
-            z_long(qp, k).start()
-        for k in range(NY):
-            z_long(qp, k).wait_recv()
-            z_short(qm, k).wait_recv()
-            zsum[qo, k] = (
-                zsum[qo, k].astype(F32) + zin[0, k].astype(F32) + zin[1, k].astype(F32)
-            ).astype(BF16)
-            if k > 0:
-                dt_copy(k, seq[k]).start()
-            else:
-
-                @pl.when(xl == par)
-                def _():
-                    pltpu.make_async_copy(zsum.at[qo, 0], dtin.at[xl], dt_r.at[xl]).start()
-
-                @pl.when(xl != par)
-                def _():
-                    dt_copy(0, seq[0]).start()
+        for k in groups[s]:
+            inputs_of(seq[k], k)
+        grads_of([seq[k] for k in groups[s]], False)
+        if s == 4:
+            gsend[...] = acc[1 - h].astype(BF16)
+            gcopy = remote(gsend, grecv, g_s, g_r, partner)
+            gcopy.start()
+        cores(s - 1)
+        if s > 1:
+            middle(s - 2)
+        if s > 2:
+            collect(s - 3)
+    cores(4)
+    middle(3)
+    collect(2)
+    middle(4)
+    collect(3)
+    collect(4)
 
     remote(gsend, grecv, g_s, g_r, partner).wait_recv()
     for i in range(CHUNKS):
         for k in range(2):
             a = pl.ds(rows * i + half * k, half)
-            grad_ref[k, pl.ds(half * i, half), :] = acc[h, a, :] + grecv[a, :].astype(F32)
+            grad_ref[k, pl.ds(half * i, half), :] = (
+                acc[h, a, :] + grecv[a, :].astype(F32)
+            ) * factor
 
     for s in range(2):
         remote(zsum.at[0, 0], dtin.at[s], dt_s.at[0], dt_r.at[s], sibling).wait_recv()
@@ -435,14 +477,20 @@
         xg0.wait_send()
 
     for i in range(NY):
-        cp_plus(0, i).wait_send()
         for q in range(2):
             cp_sib(q, i).wait_send()
 
-    @pl.when(r != 1)
+    @pl.when(lax.rem(r, 2) == 0)
     def _():
         for i in range(NY):
-            cp_minus(0, i).wait_send()
+            cp_plus(0, i, 0).wait_send()
+            cp_plus(0, i, 1).wait_send()
+            cp_minus(0, i, 0).wait_send()
+
+    @pl.when(r == 0)
+    def _():
+        for i in range(NY):
+            cp_minus(0, i, 1).wait_send()
 
     for s in range(4):
         for d in range(2):
@@ -454,23 +502,44 @@
     for k in range(NY):
         for q in range(2):
             sib_copy(q, seq[k], k).wait_send()
-        z_long(0, k).wait_send()
-
-    @pl.when(r != 0)
+
+    @pl.when(lax.rem(r, 2) == 1)
     def _():
         for k in range(NY):
-            z_short(0, k).wait_send()
+            z_copy(0, 0, k).wait_send()
+            z_copy(0, 1, k).wait_send()
+
+    @pl.when(lax.rem(r, 2) == 0)
+    def _():
+        for k in range(NY):
+            z_copy(0, 2, k).wait_send()
+
+    @pl.when(r == 2)
+    def _():
+        for k in range(NY):
+            z_copy(0, 3, k).wait_send()
 
     @pl.when(r == 0)
     def _():
         for k in range(1, NY):
-            dt_copy(k, seq[k]).wait_send()
+            dt_copy(k).wait_send()
 
     @pl.when(jnp.logical_and(r == 0, xl != par))
     def _():
-        dt_copy(0, seq[0]).wait_send()
+        dt_copy(0).wait_send()
 
     gcopy.wait_send()
+
+
+def write_out(a_ref, b_ref, c_ref, ao_ref, bo_ref, co_ref, sem):
+    copies = [
+        pltpu.make_async_copy(src, dst, sem.at[i])
+        for i, (src, dst) in enumerate(((c_ref, co_ref), (a_ref, ao_ref), (b_ref, bo_ref)))
+    ]
+    for copy in copies:
+        copy.start()
+    for copy in copies:
+        copy.wait()
 
 
 def body(tokens, codes, scales, d_hidden):
@@ -478,7 +547,6 @@
     _, wrows, group = codes.shape
     all2 = 2 * group
     codes_t = jnp.transpose(codes, (0, 2, 1))
-    scale_t = jnp.transpose(scales, (0, 2, 1)).astype(F32)
     dh_t = jnp.transpose(d_hidden)
     dma = pltpu.SemaphoreType.DMA
     vm = pl.BlockSpec(memory_space=pltpu.VMEM)
@@ -489,9 +557,13 @@
             jax.ShapeDtypeStruct((t, dloc), BF16),
             jax.ShapeDtypeStruct((2, group, wrows), F32),
         ),
-        in_specs=[vm] * 4,
+        in_specs=[pl.BlockSpec(memory_space=pltpu.HBM)] * 4,
         out_specs=(vm, vm, vm),
         scratch_shapes=[
+            pltpu.VMEM((2, group, wrows), BF16),
+            pltpu.VMEM(scales.shape, BF16),
+            pltpu.VMEM((group, t), BF16),
+            pltpu.SemaphoreType.DMA((4,)),
             pltpu.VMEM((t, dloc), BF16),
             pltpu.VMEM((4, NY, t, dloc), BF16),
             pltpu.VMEM((2, all2, wrows), BF16),
@@ -504,7 +576,7 @@
             pltpu.VMEM((2, all2, wrows), F32),
             pltpu.VMEM((4, NY, dloc, t), BF16),
             pltpu.VMEM((2, NY, dloc, t), BF16),
-            pltpu.VMEM((2, NY, dloc, t), BF16),
+            pltpu.VMEM((4, NY, dloc, t), BF16),
             pltpu.VMEM((2, NY, dloc, t), BF16),
             pltpu.VMEM((2, dloc, t), BF16),
             pltpu.VMEM((all2, wrows), BF16),
@@ -514,9 +586,9 @@
             dma(()),
             dma((2,)),
             dma((NY,)),
+            dma((2, NY)),
             dma((NY,)),
-            dma((NY,)),
-            dma((NY,)),
+            dma((2, NY)),
             dma((NY,)),
             dma((2, NY)),
             dma((2, NY)),
@@ -526,19 +598,24 @@
             dma((4, 2, CHUNKS)),
             dma((2, NY)),
             dma((2, NY)),
-            dma((NY,)),
-            dma((NY,)),
-            dma((NY,)),
-            dma((NY,)),
+            dma((4, NY)),
+            dma((4, NY)),
             dma((NY,)),
             dma((2,)),
             dma(()),
             dma(()),
         ],
-        compiler_params=pltpu.CompilerParams(collective_id=0, has_side_effects=True),
-    )(tokens, codes_t, scale_t, dh_t)
-    factor = 1.0 / math.sqrt(t * lax.axis_size("local"))
-    return (jnp.transpose(hid_t), dtok, jnp.transpose(grad_t, (0, 2, 1)) * factor)
+        compiler_params=pltpu.CompilerParams(collective_id=0, has_side_effects=True, vmem_limit_bytes=24 * 1024 * 1024),
+    )(*(pltpu.with_memory_space_constraint(a, pltpu.HBM) for a in (tokens, codes_t, scales, dh_t)))
+    hid_t, dtok, grad_t = pl.pallas_call(
+        write_out,
+        out_shape=tuple(jax.ShapeDtypeStruct(a.shape, a.dtype) for a in (hid_t, dtok, grad_t)),
+        in_specs=[vm] * 3,
+        out_specs=(pl.BlockSpec(memory_space=pltpu.HBM),) * 3,
+        scratch_shapes=[dma((3,))],
+        compiler_params=pltpu.CompilerParams(vmem_limit_bytes=4 * 1024 * 1024),
+    )(hid_t, dtok, grad_t)
+    return (jnp.transpose(hid_t), dtok, jnp.transpose(grad_t, (0, 2, 1)))
 
 
 def solution(mesh):

time: 114 us -> 93.7 us (0.82)
  the two profiles are of different devices: /device:TPU:126 before, /device:TPU:1 now
where the time goes in v2:
time: 93.7 us; the launch traced here: 93.6 us
  Pallas kernels  92.9 us (99%)
    pallas_call x1, Pallas kernels, body(): pl.pallas_call(kernel, out_shape=(jax.ShapeDtypeStruct((group, t), BF16),...  91.9 us

profile of v2, /device:TPU:1, one launch (start us, length us, event | category | flops | bytes accessed | tf_op | source)
XLA Modules:
  0.0 93.6 jit_solution(2759024451707521406)
XLA Ops:
  0.6 91.9 %shard_map.67 = (bf16[448,128]{1,0:T(8,128)(2,1)S(1)}, bf16[128,128]{1,0:T(8,128)(2,1)S(1)}, f32[2,448,256]{2,1,0:T(8,128)S(1)}) custom-call(bf16[128,128]{1,0:T(8,128)(2,1)} %tok_hbm.1, bf16[2,448,256]{2,1,0:T(8,128)(2,1)} %bitcast.4, bf16[2,2,448]{2,1,0:T(2,128)(2,1)} %scale_hbm.1, bf16[448,128]{1,0:T(8,128)(2,1)} %bitcast.5), custom_call_target="tpu_custom_call" | custom-call | tf_op jit(solution)/shard_map/pallas_call | solution.py:553
  92.6 1.0 %shard_map.68 = (bf16[448,128]{1,0:T(8,128)(2,1)}, bf16[128,128]{1,0:T(8,128)(2,1)}, f32[2,448,256]{2,1,0:T(8,128)}) custom-call(bf16[448,128]{1,0:T(8,128)(2,1)S(1)} %get-tuple-element.9.a_ref, bf16[128,128]{1,0:T(8,128)(2,1)S(1)} %get-tuple-element.10.b_ref, f32[2,448,256]{2,1,0:T(8,128)S(1)} %get-tuple-element.11.c_ref), custom_call_target="tpu_custom_call" | custom-call | tf_op jit(solution)/shard_map/pallas_call | solution.py:610

commit v3 on v2

--- a/solution.py
+++ b/solution.py
@@ -130,32 +130,10 @@
             src_ref=src, dst_ref=dst, send_sem=ss, recv_sem=rr, device_id=to, device_id_type=MESH
         )
 
-    loads[1].wait()
-    loads[2].wait()
-    pick = (
-        lax.broadcasted_iota(jnp.int32, (2, 2 * BLOCK), 1) // BLOCK
-        == lax.broadcasted_iota(jnp.int32, (2, 2 * BLOCK), 0)
-    ).astype(F32)
-    for k in range(2):
-        spread = lax.dot_general(
-            scale_ref[k].astype(F32),
-            pick,
-            (((0,), (0,)), ((), ())),
-            precision=lax.Precision.HIGHEST,
-            preferred_element_type=F32,
-        )
-        for i in range(CHUNKS):
-            f = pl.ds(half * i, half)
-            code = codes_ref[k, f, :].astype(F32)
-            s = spread[half * i : half * (i + 1)]
-            w[h, pl.ds(rows * i + half * k, half), :] = (code * s).astype(BF16)
     loads[0].wait()
     loads[3].wait()
 
     pl.semaphore_wait(barrier, len(peers))
-
-    wcopy = remote(w.at[h], w.at[h], w_s, w_r, partner)
-    wcopy.start()
 
     ystar = 2 * lax.rem(z, 4) + xl
     qsrc = lax.div(z, 4)
@@ -175,6 +153,27 @@
     def _():
         xg0.start()
 
+    loads[1].wait()
+    loads[2].wait()
+    pick = (
+        lax.broadcasted_iota(jnp.int32, (2, 2 * BLOCK), 1) // BLOCK
+        == lax.broadcasted_iota(jnp.int32, (2, 2 * BLOCK), 0)
+    ).astype(BF16)
+    for k in range(2):
+        spread = lax.dot_general(
+            scale_ref[k],
+            pick,
+            (((0,), (0,)), ((), ())),
+            preferred_element_type=F32,
+        )
+        for i in range(CHUNKS):
+            f = pl.ds(half * i, half)
+            code = codes_ref[k, f, :].astype(F32)
+            s = spread[half * i : half * (i + 1)]
+            w[h, pl.ds(rows * i + half * k, half), :] = (code * s).astype(BF16)
+    wcopy = remote(w.at[h], w.at[h], w_s, w_r, partner)
+    wcopy.start()
+
     dz = lax.rem(z - lax.div(y, 2) + NZ, NZ)
     r = lax.rem(dz, 4)
     qo = lax.div(dz, 4)
@@ -232,6 +231,7 @@
 
     stages = ((0,), (1, 2), (3, 4), (5, 6, 7))
     early = ((0, 1, 2), (3, 4), (5, 6), (7,))
+    ahead = ((0, 1, 2), (3,), (), ())
 
     def tokens_stage(t):
         @pl.when(r == 0)
@@ -251,7 +251,7 @@
 
         @pl.when(r == 2)
         def _():
-            for i in stages[t]:
+            for i in ahead[t]:
                 relay(i)
 
         @pl.when(r == 3)
@@ -309,6 +309,13 @@
                 rs_copy(s - 1, d, i).wait_recv()
                 rs[d, s - 1, ch(i)] = (rs[d, s - 1, ch(i)].astype(F32) + part[d, ch(i)]).astype(BF16)
                 rs_copy(s, d, i).start()
+            nxt = {(1, 0): 4, (1, 2): 5, (2, 0): 6, (2, 2): 7}.get((s, i))
+            if nxt is not None:
+
+                @pl.when(r == 2)
+                def _():
+                    relay(nxt)
+
     own[...] = partial(y, 0, CHUNKS)
 
     def ag_copy(s, d, i):

time: 93.7 us -> 88.5 us (0.945)
  Pallas kernels: 92.9 us -> 87.3 us
    pallas_call x1, Pallas kernels: 91.9 us -> 86.3 us  [body(): pl.pallas_call(kernel, out_shape=(jax.ShapeDtypeStruct((group, t), BF16),...]
where the time goes in v3:
time: 88.5 us; the launch traced here: 87.9 us
  Pallas kernels  87.3 us (99%)
    pallas_call x1, Pallas kernels, body(): pl.pallas_call(kernel, out_shape=(jax.ShapeDtypeStruct((group, t), BF16),...  86.3 us

profile of v3, /device:TPU:1, one launch (start us, length us, event | category | flops | bytes accessed | tf_op | source)
XLA Modules:
  0.0 87.9 jit_solution(16865672731653901239)
XLA Ops:
  0.6 86.3 %shard_map.67 = (bf16[448,128]{1,0:T(8,128)(2,1)S(1)}, bf16[128,128]{1,0:T(8,128)(2,1)S(1)}, f32[2,448,256]{2,1,0:T(8,128)S(1)}) custom-call(bf16[128,128]{1,0:T(8,128)(2,1)} %tok_hbm.1, bf16[2,448,256]{2,1,0:T(8,128)(2,1)} %bitcast.4, bf16[2,2,448]{2,1,0:T(2,128)(2,1)} %scale_hbm.1, bf16[448,128]{1,0:T(8,128)(2,1)} %bitcast.5), custom_call_target="tpu_custom_call" | custom-call | tf_op jit(solution)/shard_map/pallas_call | solution.py:560
  87.0 1.0 %shard_map.68 = (bf16[448,128]{1,0:T(8,128)(2,1)}, bf16[128,128]{1,0:T(8,128)(2,1)}, f32[2,448,256]{2,1,0:T(8,128)}) custom-call(bf16[448,128]{1,0:T(8,128)(2,1)S(1)} %get-tuple-element.9.a_ref, bf16[128,128]{1,0:T(8,128)(2,1)S(1)} %get-tuple-element.10.b_ref, f32[2,448,256]{2,1,0:T(8,128)S(1)} %get-tuple-element.11.c_ref), custom_call_target="tpu_custom_call" | custom-call | tf_op jit(solution)/shard_map/pallas_call | solution.py:617

commit v4 on v3

--- a/solution.py
+++ b/solution.py
@@ -49,6 +49,7 @@
     dp,
     sib,
     zin,
+    zx,
     zsum,
     dtin,
     gsend,
@@ -72,6 +73,8 @@
     sb_r,
     zo_s,
     zo_r,
+    zx_s,
+    zx_r,
     dt_s,
     dt_r,
     g_s,
@@ -118,6 +121,8 @@
 
     barrier = pltpu.get_barrier_semaphore()
     peers = [up_z, dn_z, up_z2, dn_z2, sibling, partner]
+    cross = [dev(z_, xl, other, h, y) for z_ in (zd, zu, zd2, zu2)]
+    peers += cross
     for dx in range(2):
         for dy in range(NY):
             if dx or dy:
@@ -287,17 +292,15 @@
     def firsts(d):
         return range(hc) if d == 0 else range(hc, CHUNKS)
 
-    p0 = partial(block(4), 0, CHUNKS)
     for d in range(2):
-        rs0[d] = p0[d * hc * rows : (d + 1) * hc * rows].astype(BF16)
+        rs0[d] = partial(block(4), d * hc, (d + 1) * hc).astype(BF16)
         for i in firsts(d):
             rs_copy(0, d, i).start()
     for s in range(1, 4):
         tokens_stage(s)
         for d in range(2):
             part[d] = partial(block(4 - s if d == 0 else s - 4), 0, CHUNKS)
-        if s == 1:
-            for d in range(2):
+            if s == 1:
                 for i in firsts(1 - d):
                     rs[d, 0, ch(i)] = part[d, ch(i)].astype(BF16)
                     rs_copy(1, d, i).start()
@@ -370,6 +373,9 @@
             v = dot_nn(wt[q], dg[b]).astype(BF16)
             dp[2 * q, b] = v[:128]
             dp[2 * q + 1, b] = v[128:]
+        if k == 7:
+            last_leaves()
+        for q in range(2):
             sib_copy(q, b, k).start()
 
     seq = [block(d) for d in (0, -1, 1, -2, 2, -3, 3, 4)]
@@ -381,17 +387,42 @@
     def z_copy(q, w_, k):
         return remote(zsum.at[q, k], zin.at[w_, k], zo_s.at[w_, k], zo_r.at[w_, k], z_to[w_])
 
-    def z_add(q, ways, k):
+    def z_add(q, ways, k, crossed=()):
         v = zsum[q, k].astype(F32)
         for w_ in ways:
             z_copy(q, w_, k).wait_recv()
             v = v + zin[w_, k].astype(F32)
+        for w_ in crossed if k == 7 else ():
+            z_cross(q, w_).wait_recv()
+            v = v + zx[w_].astype(F32)
         zsum[q, k] = v.astype(BF16)
 
     def dt_copy(k):
         return remote(
             zsum.at[qo, k], dtin.at[xl], dt_s.at[k], dt_r.at[xl], dev(z, par, c, h, seq[k])
         )
+
+    def z_direct(q, w_):
+        return remote(
+            dp.at[2 * q + c, seq[7]], zin.at[w_, 7], zo_s.at[w_, 7], zo_r.at[w_, 7], z_to[w_]
+        )
+
+    def z_cross(q, w_):
+        return remote(
+            dp.at[2 * q + other, seq[7]], zx.at[w_], zx_s.at[w_], zx_r.at[w_], cross[w_]
+        )
+
+    def last_leaves():
+        @pl.when(lax.rem(r, 2) == 1)
+        def _():
+            for q, w_ in ((qp, 0), (qm, 1)):
+                z_direct(q, w_).start()
+                z_cross(q, w_).start()
+
+        @pl.when(r == 0)
+        def _():
+            z_direct(qp, 2).start()
+            z_cross(qp, 2).start()
 
     def cores(g):
         for k in groups[g]:
@@ -400,6 +431,9 @@
                 v = dp[2 * q + c, seq[k]].astype(F32) + sib[q, k].astype(F32)
                 zsum[q, k] = v.astype(BF16)
 
+            if k == 7:
+                continue
+
             @pl.when(lax.rem(r, 2) == 1)
             def _():
                 z_copy(qp, 0, k).start()
@@ -413,16 +447,16 @@
         @pl.when(r == 2)
         def _():
             for k in groups[g]:
-                z_add(qp, (0, 2), k)
+                z_add(qp, (0, 2), k, (0, 2))
                 z_copy(qp, 2, k).start()
-                z_add(qm, (1,), k)
+                z_add(qm, (1,), k, (1,))
                 z_copy(qm, 3, k).start()
 
     def collect(g):
         @pl.when(r == 0)
         def _():
             for k in groups[g]:
-                z_add(qo, (0, 1, 2, 3), k)
+                z_add(qo, (0, 1, 2, 3), k, (0, 1))
                 if k > 0:
                     dt_copy(k).start()
                 else:
@@ -437,34 +471,51 @@
 
     inputs_of(seq[0], 0)
     grads_of([seq[0]], True)
-    for s in range(1, 5):
+    def g_copy(i):
+        return remote(gsend.at[ch(i)], grecv.at[ch(i)], g_s.at[i], g_r.at[i], partner)
+
+    for s in range(1, 4):
         for i in range(CHUNKS):
             for d in range(2):
-                if s < 4 or i in firsts(d):
-                    ag_wait(s - 1, d, i)
-                if s < 3 or (s == 3 and i in firsts(d)):
+                ag_wait(s - 1, d, i)
+                if s < 3 or i in firsts(d):
                     ag_copy(s, d, i).start()
+            if i == 1:
+                cores(s - 1)
         for k in groups[s]:
             inputs_of(seq[k], k)
         grads_of([seq[k] for k in groups[s]], False)
-        if s == 4:
-            gsend[...] = acc[1 - h].astype(BF16)
-            gcopy = remote(gsend, grecv, g_s, g_r, partner)
-            gcopy.start()
-        cores(s - 1)
+        middle(s - 1)
         if s > 1:
-            middle(s - 2)
-        if s > 2:
-            collect(s - 3)
+            collect(s - 2)
+
+    def send_grads(i):
+        pair = jnp.concatenate([x[2 * (1 - h) + j, seq[7]] for j in range(2)], axis=1)
+        v = dot_nn(dg[seq[7], ch(i)], pair)
+        gsend[ch(i)] = (acc[1 - h, ch(i)] + v).astype(BF16)
+        g_copy(i).start()
+
+    for i in range(hc):
+        ag_wait(3, 0, i)
+        ag_wait(3, 1, i + hc)
+        if i == hc - 1:
+            inputs_of(seq[7], 7)
+        send_grads(i)
+        send_grads(i + hc)
+        if i == 0:
+            cores(3)
+    collect(2)
     cores(4)
+    for j in range(2):
+        col = slice(128 * j, 128 * j + 128)
+        acc[h, :, col] = acc[h, :, col] + dot_nn(dg[seq[7]], x[2 * h + j, seq[7]])
     middle(3)
-    collect(2)
     middle(4)
     collect(3)
     collect(4)
 
-    remote(gsend, grecv, g_s, g_r, partner).wait_recv()
     for i in range(CHUNKS):
+        g_copy(i).wait_recv()
         for k in range(2):
             a = pl.ds(rows * i + half * k, half)
             grad_ref[k, pl.ds(half * i, half), :] = (
@@ -515,6 +566,8 @@
         for k in range(NY):
             z_copy(0, 0, k).wait_send()
             z_copy(0, 1, k).wait_send()
+        z_cross(0, 0).wait_send()
+        z_cross(0, 1).wait_send()
 
     @pl.when(lax.rem(r, 2) == 0)
     def _():
@@ -528,6 +581,7 @@
 
     @pl.when(r == 0)
     def _():
+        z_cross(0, 2).wait_send()
         for k in range(1, NY):
             dt_copy(k).wait_send()
 
@@ -535,7 +589,8 @@
     def _():
         dt_copy(0).wait_send()
 
-    gcopy.wait_send()
+    for i in range(CHUNKS):
+        g_copy(i).wait_send()
 
 
 def write_out(a_ref, b_ref, c_ref, ao_ref, bo_ref, co_ref, sem):
@@ -584,6 +639,7 @@
             pltpu.VMEM((4, NY, dloc, t), BF16),
             pltpu.VMEM((2, NY, dloc, t), BF16),
             pltpu.VMEM((4, NY, dloc, t), BF16),
+            pltpu.VMEM((3, dloc, t), BF16),
             pltpu.VMEM((2, NY, dloc, t), BF16),
             pltpu.VMEM((2, dloc, t), BF16),
             pltpu.VMEM((all2, wrows), BF16),
@@ -607,10 +663,12 @@
             dma((2, NY)),
             dma((4, NY)),
             dma((4, NY)),
+            dma((3,)),
+            dma((3,)),
             dma((NY,)),
             dma((2,)),
-            dma(()),
-            dma(()),
+            dma((CHUNKS,)),
+            dma((CHUNKS,)),
         ],
         compiler_params=pltpu.CompilerParams(collective_id=0, has_side_effects=True, vmem_limit_bytes=24 * 1024 * 1024),
     )(*(pltpu.with_memory_space_constraint(a, pltpu.HBM) for a in (tokens, codes_t, scales, dh_t)))

time: 88.5 us -> 87.6 us (0.990)
  Pallas kernels: 87.3 us -> 86.3 us
    pallas_call x1, Pallas kernels: 86.3 us -> 85.3 us  [body(): pl.pallas_call(kernel, out_shape=(jax.ShapeDtypeStruct((group, t), BF16),...]
where the time goes in v4:
time: 87.6 us; the launch traced here: 87 us
  Pallas kernels  86.3 us (99%)
    pallas_call x1, Pallas kernels, body(): pl.pallas_call(kernel, out_shape=(jax.ShapeDtypeStruct((group, t), BF16),...  85.3 us

profile of v4, /device:TPU:1, one launch (start us, length us, event | category | flops | bytes accessed | tf_op | source)
XLA Modules:
  0.0 87.0 jit_solution(6652022970630567446)
XLA Ops:
  0.6 85.3 %shard_map.67 = (bf16[448,128]{1,0:T(8,128)(2,1)S(1)}, bf16[128,128]{1,0:T(8,128)(2,1)S(1)}, f32[2,448,256]{2,1,0:T(8,128)S(1)}) custom-call(bf16[128,128]{1,0:T(8,128)(2,1)} %tok_hbm.1, bf16[2,448,256]{2,1,0:T(8,128)(2,1)} %bitcast.4, bf16[2,2,448]{2,1,0:T(2,128)(2,1)} %scale_hbm.1, bf16[448,128]{1,0:T(8,128)(2,1)} %bitcast.5), custom_call_target="tpu_custom_call" | custom-call | tf_op jit(solution)/shard_map/pallas_call | solution.py:615
  86.0 1.0 %shard_map.68 = (bf16[448,128]{1,0:T(8,128)(2,1)}, bf16[128,128]{1,0:T(8,128)(2,1)}, f32[2,448,256]{2,1,0:T(8,128)}) custom-call(bf16[448,128]{1,0:T(8,128)(2,1)S(1)} %get-tuple-element.9.a_ref, bf16[128,128]{1,0:T(8,128)(2,1)S(1)} %get-tuple-element.10.b_ref, f32[2,448,256]{2,1,0:T(8,128)S(1)} %get-tuple-element.11.c_ref), custom_call_target="tpu_custom_call" | custom-call | tf_op jit(solution)/shard_map/pallas_call | solution.py:675

commit v5 on v4

--- a/solution.py
+++ b/solution.py
@@ -506,13 +506,13 @@
             cores(3)
     collect(2)
     cores(4)
-    for j in range(2):
-        col = slice(128 * j, 128 * j + 128)
-        acc[h, :, col] = acc[h, :, col] + dot_nn(dg[seq[7]], x[2 * h + j, seq[7]])
     middle(3)
     middle(4)
     collect(3)
     collect(4)
+    for j in range(2):
+        col = slice(128 * j, 128 * j + 128)
+        acc[h, :, col] = acc[h, :, col] + dot_nn(dg[seq[7]], x[2 * h + j, seq[7]])
 
     for i in range(CHUNKS):
         g_copy(i).wait_recv()

time: 87.6 us -> 87.6 us (level)
  no operation moved by 1% of the time
where the time goes in v5:
time: 87.6 us; the launch traced here: 87 us
  Pallas kernels  86.3 us (99%)
    pallas_call x1, Pallas kernels, body(): pl.pallas_call(kernel, out_shape=(jax.ShapeDtypeStruct((group, t), BF16),...  85.3 us

profile of v5, /device:TPU:1, one launch (start us, length us, event | category | flops | bytes accessed | tf_op | source)
XLA Modules:
  0.0 87.0 jit_solution(12044479670177943208)
XLA Ops:
  0.6 85.3 %shard_map.67 = (bf16[448,128]{1,0:T(8,128)(2,1)S(1)}, bf16[128,128]{1,0:T(8,128)(2,1)S(1)}, f32[2,448,256]{2,1,0:T(8,128)S(1)}) custom-call(bf16[128,128]{1,0:T(8,128)(2,1)} %tok_hbm.1, bf16[2,448,256]{2,1,0:T(8,128)(2,1)} %bitcast.4, bf16[2,2,448]{2,1,0:T(2,128)(2,1)} %scale_hbm.1, bf16[448,128]{1,0:T(8,128)(2,1)} %bitcast.5), custom_call_target="tpu_custom_call" | custom-call | tf_op jit(solution)/shard_map/pallas_call | solution.py:615
  86.0 1.0 %shard_map.68 = (bf16[448,128]{1,0:T(8,128)(2,1)}, bf16[128,128]{1,0:T(8,128)(2,1)}, f32[2,448,256]{2,1,0:T(8,128)}) custom-call(bf16[448,128]{1,0:T(8,128)(2,1)S(1)} %get-tuple-element.9.a_ref, bf16[128,128]{1,0:T(8,128)(2,1)S(1)} %get-tuple-element.10.b_ref, f32[2,448,256]{2,1,0:T(8,128)S(1)} %get-tuple-element.11.c_ref), custom_call_target="tpu_custom_call" | custom-call | tf_op jit(solution)/shard_map/pallas_call | solution.py:675
